TPU v7x, 256 devices: a whole 4x4x8 slice. The times are simulated.
256 devices in a mesh: tok: 16 (over y, x), feat: 16 (over z, core).
Axes of the slice: x: 4, y: 4, z: 8, core: 2. Of those that a mesh axis runs over, the one named last changes fastest.
Arguments:
- calib: float32 [16384, 22016], P('tok', 'feat')
- teacher_w: bfloat16 [22016, 256], P('feat'), may hold values from -6 to 6
- mask: int32 [172, 2], replicated, may hold values from 0 to 1, as said below
Outputs:
- solution: float32 [22016, 256], P('feat')
- residual: float32 [22016, 256], P('feat')
Inputs may be any that keep to these rules, and one draw needn't show every extreme that they name: `mask`: every column block has at least one row block with 1.
All inputs are finite; a program needn't handle non-finite values.
Results may differ from a plain program's by a relative error of at most 0.0003.
Values sent between devices are 32-bit elements; how exact they have to be, the bound alone decides.
No kernel may reach another device: no remote copies, remote signals or barrier semaphores. Data moves between devices by JAX's collectives and lax.ppermute only.
A program may use at most 64 MiB of HBM per device.

v0:
```python
import jax
import jax.numpy as jnp
from jax import lax
from jax.sharding import PartitionSpec as P

BLOCK = 128
ITERS = 2
DAMP_REL = 0.2


def matmul(left, right):
    return jnp.dot(left, right, precision=lax.Precision.HIGHEST, preferred_element_type=jnp.float32)


def back_product(left, right):
    return lax.dot_general(
        left,
        right,
        (((0,), (0,)), ((), ())),
        precision=lax.Precision.HIGHEST,
        preferred_element_type=jnp.float32,
    )


def col_norm(values):
    return lax.psum(jnp.sum(values * values, axis=0), "feat")


def on_device(calib, teacher_w, mask):
    feat_count = lax.axis_size("feat")
    feat_place = lax.axis_index("feat")
    rows_dev = calib.shape[0]
    din_dev = calib.shape[1]
    share = rows_dev // feat_count
    first_row = feat_place * din_dev
    block_ids = (first_row + jnp.arange(din_dev, dtype=jnp.int32)) // BLOCK
    onehot = (block_ids[:, None] == jnp.arange(mask.shape[0], dtype=jnp.int32)[None, :]).astype(
        jnp.float32
    )
    live_blocks = matmul(onehot, mask.astype(jnp.float32))
    live = jnp.repeat(live_blocks, BLOCK, axis=1)
    total = lax.psum(jnp.sum(calib * calib), ("tok", "feat"))
    damp = DAMP_REL * total / (din_dev * feat_count)

    def gram(vec):
        rows_out = lax.psum(matmul(calib, vec), "feat")
        partial_back = back_product(calib, rows_out)
        own_rows = lax.dynamic_slice_in_dim(rows_out, feat_place * share, share, 0)
        summed = lax.psum(partial_back, "tok")
        return (live * summed, own_rows)

    targets, unused_rows = gram(teacher_w.astype(jnp.float32))
    solution = jnp.zeros_like(targets)
    residual = targets
    direction = targets
    norm_now = col_norm(residual)
    for step in range(ITERS):
        image_raw, own_rows = gram(direction)
        image = image_raw + damp * direction
        curvature = lax.psum(jnp.sum(direction * image, axis=0), "feat")
        alpha = norm_now / curvature
        solution = solution + alpha * direction
        residual = residual - alpha * image
        fresh = col_norm(residual)
        direction = residual + fresh / norm_now * direction
        norm_now = fresh
    return (solution, residual)


def solution(mesh):
    in_specs = (P("tok", "feat"), P("feat", None), P())
    out_specs = (P("feat", None), P("feat", None))
    return jax.shard_map(
        on_device, mesh=mesh, in_specs=in_specs, out_specs=out_specs, check_vma=False
    )
```

profile of v0, /device:TPU:1, one launch (start us, length us, event | category | flops | bytes accessed | tf_op | source)
XLA Modules:
  0.0 783.0 jit_solution(17692124888101686545)
XLA Ops:
  7.2 1.0 copy-done
  8.3 8.2 %fusion.8 = f32[1024,256]{1,0:T(8,128)} fusion(f32[1024,1376]{0,1:T(8,128)} %param.3, bf16[1376,256]{1,0:T(8,128)(2,1)S(1)} %copy-done), kind=kOutput, calls=%fused_computation.32 | convolution fusion | flops 4328521728 | bytes 7389184 | tf_op jit(solution)/shard_map/dot_general | solution.py:12
  16.6 115.3 %all-reduce.8.cloned.1.call-done = f32[1024,256]{1,0:T(8,128)} async-done(((f32[1024,256]{1,0:T(8,128)}), f32[1024,256]{1,0:T(8,128)}) %all-reduce.8.cloned.1.call-update) | async-done | bytes 1048592 | tf_op jit(solution)/shard_map/psum | solution.py:46
  131.8 8.7 %convolution_bitcast_fusion.2 = f32[1376,256]{1,0:T(8,128)} fusion(f32[1024,256]{1,0:T(8,128)} %all-reduce.8.cloned.1.call-done, f32[1024,1376]{0,1:T(8,128)} %param.3), kind=kOutput, calls=%fused_computation.3 | convolution fusion | flops 4328521728 | bytes 8093696 | tf_op jit(solution)/shard_map/dot_general | solution.py:16
  141.2 0.8 fusion.2
  142.0 95.4 %all-reduce.10.cloned.1.call-done = f32[1376,256]{1,0:T(8,128)} async-done(((f32[1376,256]{1,0:T(8,128)}), f32[1376,256]{1,0:T(8,128)}) %all-reduce.10.cloned.1.call-update) | async-done | bytes 1409040 | tf_op jit(solution)/shard_map/psum | solution.py:49
  237.4 3.1 broadcast_in_dim.2
  240.7 8.3 %convolution_bitcast_fusion.4 = f32[1024,256]{0,1:T(8,128)} fusion(f32[1376,256]{1,0:T(8,128)S(1)} %bitcast_multiply_fusion.2, f32[1024,1376]{0,1:T(8,128)} %param.3), kind=kOutput, calls=%fused_computation.20 | convolution fusion | flops 4328521728 | bytes 8093696 | tf_op jit(solution)/shard_map/dot_general | solution.py:12
  249.0 112.1 %all-reduce.12.cloned.1.call-done = f32[1024,256]{0,1:T(8,128)} async-done(((f32[1024,256]{0,1:T(8,128)}), f32[1024,256]{0,1:T(8,128)}) %all-reduce.12.cloned.1.call-update) | async-done | bytes 1048592 | tf_op jit(solution)/shard_map/psum | solution.py:46
  361.2 8.7 %convolution_bitcast_fusion.1 = f32[1376,256]{1,0:T(8,128)} fusion(f32[1024,256]{0,1:T(8,128)} %all-reduce.12.cloned.1.call-done, f32[1024,1376]{0,1:T(8,128)} %param.3), kind=kOutput, calls=%fused_computation.2 | convolution fusion | flops 4328521728 | bytes 8093696 | tf_op jit(solution)/shard_map/dot_general | solution.py:16
  369.9 4.7 multiply_reduce_fusion
  374.6 78.6 %psum.82 = f32[]{:T(128)} all-reduce(f32[]{:T(128)} %multiply_reduce_fusion), channel_id=1, replica_groups=mesh['tok'=16,'feat'=16] {'tok','feat'}, use_global_device_ids=true, to_apply=%region_7.8 | all-reduce | flops 1 | bytes 8 | tf_op jit(solution)/shard_map/psum | solution.py:42
  453.9 13.1 %all-reduce.14.cloned.1.call-done = f32[1376,256]{1,0:T(8,128)} async-done(((f32[1376,256]{1,0:T(8,128)}), f32[1376,256]{1,0:T(8,128)}) %all-reduce.14.cloned.1.call-update) | async-done | bytes 1409040 | tf_op jit(solution)/shard_map/psum | solution.py:49
  466.9 1.7 multiply_reduce_fusion.3
  468.6 25.5 %all-reduce = (f32[256]{0:T(256)S(1)}, f32[256]{0:T(256)S(1)}) all-reduce(f32[256]{0:T(256)S(1)} %get-tuple-element.3, f32[256]{0:T(256)S(1)} %get-tuple-element.2), channel_id=1, replica_groups=mesh['tok'=16,'feat'=16] {'feat'}, use_global_device_ids=true, to_apply=%region_3.4 | all-reduce | flops 512 | bytes 4096 | tf_op jit(solution)/shard_map/psum | solution.py:26
  494.1 2.8 multiply_reduce_fusion.2
  496.9 24.6 %psum.84 = f32[256]{0:T(256)S(1)} all-reduce(f32[256]{0:T(256)S(1)} %get-tuple-element.6), channel_id=1, replica_groups=mesh['tok'=16,'feat'=16] {'feat'}, use_global_device_ids=true, to_apply=%region_11.12 | all-reduce | flops 256 | bytes 2048 | tf_op jit(solution)/shard_map/psum | solution.py:26
  521.5 8.7 %convolution_bitcast_fusion.3 = f32[1024,256]{0,1:T(8,128)} fusion(f32[1024,1376]{0,1:T(8,128)} %param.3, f32[1376,256]{1,0:T(8,128)} %get-tuple-element.7, f32[1376,256]{1,0:T(8,128)S(1)} %bitcast_multiply_fusion.2, f32[256]{0:T(256)S(1)} %div.30), kind=kOutput, calls=%fused_computation.19 | convolution fusion | flops 4329226240 | bytes 9503744 | tf_op jit(solution)/shard_map/dot_general | solution.py:12
  530.2 109.2 %all-reduce.16.cloned.1.call-done = f32[1024,256]{0,1:T(8,128)} async-done(((f32[1024,256]{0,1:T(8,128)}), f32[1024,256]{0,1:T(8,128)}) %all-reduce.16.cloned.1.call-update) | async-done | bytes 1048592 | tf_op jit(solution)/shard_map/psum | solution.py:46
  639.4 8.7 %convolution_bitcast_fusion = f32[1376,256]{1,0:T(8,128)} fusion(f32[1024,256]{0,1:T(8,128)} %all-reduce.16.cloned.1.call-done, f32[1024,1376]{0,1:T(8,128)} %param.3), kind=kOutput, calls=%fused_computation.1 | convolution fusion | flops 4328521728 | bytes 8093696 | tf_op jit(solution)/shard_map/dot_general | solution.py:16
  648.1 96.8 %all-reduce.18.cloned.1.call-done = f32[1376,256]{1,0:T(8,128)} async-done(((f32[1376,256]{1,0:T(8,128)}), f32[1376,256]{1,0:T(8,128)}) %all-reduce.18.cloned.1.call-update) | async-done | bytes 1409040 | tf_op jit(solution)/shard_map/psum | solution.py:49
  745.0 2.1 multiply_reduce_fusion.1
  747.1 25.3 %psum.87 = f32[256]{0:T(256)S(1)} all-reduce(f32[256]{0:T(256)S(1)} %multiply_reduce_fusion.1), channel_id=1, replica_groups=mesh['tok'=16,'feat'=16] {'feat'}, use_global_device_ids=true, to_apply=%region_15.16 | all-reduce | flops 256 | bytes 2048 | tf_op jit(solution)/shard_map/psum | solution.py:60
  772.4 3.8 multiply_subtract_fusion
  (22 shorter events, 1.2 us)
Async XLA Ops:
  7.2 1.1 copy-start
  7.2 124.7 %all-reduce.8.cloned.1.call-start = ((), (), s32[]{:S(2)}) async-start(), calls=%async_computation | async-start | bytes 2097152 | tf_op jit(solution)/shard_map/psum | solution.py:46
  16.5 220.9 %all-reduce.10.cloned.1.call-start = ((), (), s32[]{:S(2)}) async-start(), calls=%async_computation.1 | async-start | bytes 2818048 | tf_op jit(solution)/shard_map/psum | solution.py:49
  140.5 0.7 copy-start.2
  140.5 220.6 %all-reduce.12.cloned.1.call-start = ((), (), s32[]{:S(2)}) async-start(), calls=%async_computation.2 | async-start | bytes 2097152 | tf_op jit(solution)/shard_map/psum | solution.py:46
  237.4 3.1 copy-start.1
  249.0 217.9 %all-reduce.14.cloned.1.call-start = ((), (), s32[]{:S(2)}) async-start(), calls=%async_computation.3 | async-start | bytes 2818048 | tf_op jit(solution)/shard_map/psum | solution.py:49
  369.9 269.5 %all-reduce.16.cloned.1.call-start = ((), (), s32[]{:S(2)}) async-start(), calls=%async_computation.4 | async-start | bytes 2097152 | tf_op jit(solution)/shard_map/psum | solution.py:46
  530.2 214.8 %all-reduce.18.cloned.1.call-start = ((), (), s32[]{:S(2)}) async-start(), calls=%async_computation.5 | async-start | bytes 2818048 | tf_op jit(solution)/shard_map/psum | solution.py:49
Sparse Core Ops, SparseCore 0:
  16.6 115.1 all-reduce.7
  140.7 96.6 all-reduce.9
  249.1 112.0 all-reduce.11
  370.0 96.8 all-reduce.13
  530.3 109.0 all-reduce.15
  648.2 96.6 all-reduce.17
where the time goes:
time: 784 us; the launch traced here: 783 us
  waiting for transfers between devices  542 us (69%)
  blocking collectives  154 us (20%)
  matrix products  52 us (7%)
  other arithmetic  15.3 us (2%)
  between operations  14.8 us (2%)
    psum x3, waiting for transfers between devices, gram(): rows_out = lax.psum(matmul(calib, vec), 'feat')  337 us
    psum x3, waiting for transfers between devices, gram(): summed = lax.psum(partial_back, 'tok')  205 us
    psum x1, blocking collectives, on_device(): total = lax.psum(jnp.sum(calib * calib), ('tok', 'feat'))  78.6 us
    psum x2, blocking collectives, col_norm(): return lax.psum(jnp.sum(values * values, axis=0), 'feat')  50.1 us
    dot_general x3, matrix products, back_product(): lax.dot_general(left, right, (((0,), (0,)), ((), ())), precision=lax.Prec...  26 us
    dot_general x4, matrix products, matmul(): jnp.dot(left, right, precision=lax.Precision.HIGHEST, preferred_element_t...  25.9 us
    psum x1, blocking collectives, on_device(): curvature = lax.psum(jnp.sum(direction * image, axis=0), 'feat')  25.3 us
  transfers between devices with their start and end apart: 6, of which 6 were waited for; matrix products, arithmetic and copies ran while one was open for 1% of the time, Pallas kernels for 0%

commit v1 on v0

--- a/solution.py
+++ b/solution.py
@@ -46,7 +46,9 @@
         rows_out = lax.psum(matmul(calib, vec), "feat")
         partial_back = back_product(calib, rows_out)
         own_rows = lax.dynamic_slice_in_dim(rows_out, feat_place * share, share, 0)
-        summed = lax.psum(partial_back, "tok")
+        summed = partial_back
+        for hop in (1, 2, 4, 8):
+            summed = summed + lax.ppermute(summed, "tok", [(dev, dev ^ hop) for dev in range(16)])
         return (live * summed, own_rows)
 
     targets, unused_rows = gram(teacher_w.astype(jnp.float32))

time: 784 us -> 950 us (1.21)
  waiting for transfers between devices: 542 us -> 662 us
  blocking collectives: 154 us -> 179 us
  starting transfers between devices: 0.43 us -> 25 us
    ppermute x0 -> x12, waiting for transfers between devices: none -> 322 us  [gram(): lax.ppermute(summed, 'tok', [(dev, dev ^ hop) for dev in range(16)])]
    psum x3 -> x0, waiting for transfers between devices: 205 us -> none  [gram(): summed = lax.psum(partial_back, 'tok')]
    ppermute x0 -> x12, starting transfers between devices: none -> 24.9 us  [gram(): lax.ppermute(summed, 'tok', [(dev, dev ^ hop) for dev in range(16)])]
    psum x1, blocking collectives: 78.6 us -> 101 us  [on_device(): total = lax.psum(jnp.sum(calib * calib), ('tok', 'feat'))]
  transfers between devices with their start and end apart: 6 -> 15, of which waited for: 6 -> 14; matrix products, arithmetic and copies ran while one was open for 1% -> 0% of each run, Pallas kernels for 0% -> 0%
where the time goes in v1:
time: 950 us; the launch traced here: 949 us
  waiting for transfers between devices  662 us (70%)
  blocking collectives  179 us (19%)
  matrix products  45.6 us (5%)
  starting transfers between devices  25 us (3%)
  other arithmetic  17.2 us (2%)
  between operations  14.6 us (2%)
    psum x3, waiting for transfers between devices, gram(): rows_out = lax.psum(matmul(calib, vec), 'feat')  340 us
    ppermute x12, waiting for transfers between devices, gram(): lax.ppermute(summed, 'tok', [(dev, dev ^ hop) for dev in range(16)])  322 us
    psum x1, blocking collectives, on_device(): total = lax.psum(jnp.sum(calib * calib), ('tok', 'feat'))  101 us
    psum x2, blocking collectives, col_norm(): return lax.psum(jnp.sum(values * values, axis=0), 'feat')  49 us
    psum x1, blocking collectives, on_device(): curvature = lax.psum(jnp.sum(direction * image, axis=0), 'feat')  29.2 us
    ppermute x12, starting transfers between devices, gram(): lax.ppermute(summed, 'tok', [(dev, dev ^ hop) for dev in range(16)])  24.9 us
    dot_general x4, matrix products, matmul(): jnp.dot(left, right, precision=lax.Precision.HIGHEST, preferred_element_t...  24.9 us
    dot_general x3, matrix products, back_product(): lax.dot_general(left, right, (((0,), (0,)), ((), ())), precision=lax.Prec...  20.7 us
  transfers between devices with their start and end apart: 15, of which 14 were waited for; matrix products, arithmetic and copies ran while one was open for 0% of the time, Pallas kernels for 0%

profile of v1, /device:TPU:1, one launch (start us, length us, event | category | flops | bytes accessed | tf_op | source)
XLA Modules:
  0.0 949.0 jit_solution(10649312876611879514)
XLA Ops:
  8.3 8.2 fusion.9
  16.6 115.3 %all-reduce.5.cloned.1.call-done = f32[1024,256]{1,0:T(8,128)} async-done(((f32[1024,256]{1,0:T(8,128)}), f32[1024,256]{1,0:T(8,128)}) %all-reduce.5.cloned.1.call-update) | async-done | bytes 1048592 | tf_op jit(solution)/shard_map/psum | solution.py:46
  131.8 6.9 convolution_bitcast_fusion.2
  140.0 30.4 %collective-permute-done = f32[1376,256]{1,0:T(8,128)S(1)} collective-permute-done((f32[1376,256]{1,0:T(8,128)S(1)}, f32[1376,256]{1,0:T(8,128)S(1)}, u32[]{:S(2)}, u32[]{:S(2)}) %collective-permute-start) | collective-permute-done | bytes 1409056 | tf_op jit(solution)/shard_map/ppermute | solution.py:51
  173.4 29.4 %collective-permute-done.1 = f32[1376,256]{1,0:T(8,128)S(1)} collective-permute-done((f32[1376,256]{1,0:T(8,128)S(1)}, f32[1376,256]{1,0:T(8,128)S(1)}, u32[]{:S(2)}, u32[]{:S(2)}) %collective-permute-start.1) | collective-permute-done | bytes 1409056 | tf_op jit(solution)/shard_map/ppermute | solution.py:51
  204.3 28.5 %collective-permute-done.2 = f32[1376,256]{1,0:T(8,128)S(1)} collective-permute-done((f32[1376,256]{1,0:T(8,128)S(1)}, f32[1376,256]{1,0:T(8,128)S(1)}, u32[]{:S(2)}, u32[]{:S(2)}) %collective-permute-start.2) | collective-permute-done | bytes 1409056 | tf_op jit(solution)/shard_map/ppermute | solution.py:51
  237.5 27.5 %collective-permute-done.3 = f32[1376,256]{1,0:T(8,128)} collective-permute-done((f32[1376,256]{1,0:T(8,128)S(1)}, f32[1376,256]{1,0:T(8,128)}, u32[]{:S(2)}, u32[]{:S(2)}) %collective-permute-start.3) | collective-permute-done | bytes 1409056 | tf_op jit(solution)/shard_map/ppermute | solution.py:51
  270.9 6.4 convolution_bitcast_fusion.4
  277.3 117.2 %all-reduce.7.cloned.1.call-done = f32[1024,256]{0,1:T(8,128)} async-done(((f32[1024,256]{0,1:T(8,128)}), f32[1024,256]{0,1:T(8,128)}) %all-reduce.7.cloned.1.call-update) | async-done | bytes 1048592 | tf_op jit(solution)/shard_map/psum | solution.py:46
  394.5 6.9 convolution_bitcast_fusion.1
  402.7 30.4 %collective-permute-done.4 = f32[1376,256]{1,0:T(8,128)S(1)} collective-permute-done((f32[1376,256]{1,0:T(8,128)S(1)}, f32[1376,256]{1,0:T(8,128)S(1)}, u32[]{:S(2)}, u32[]{:S(2)}) %collective-permute-start.4) | collective-permute-done | bytes 1409056 | tf_op jit(solution)/shard_map/ppermute | solution.py:51
  436.0 29.4 %collective-permute-done.5 = f32[1376,256]{1,0:T(8,128)S(1)} collective-permute-done((f32[1376,256]{1,0:T(8,128)S(1)}, f32[1376,256]{1,0:T(8,128)S(1)}, u32[]{:S(2)}, u32[]{:S(2)}) %collective-permute-start.5) | collective-permute-done | bytes 1409056 | tf_op jit(solution)/shard_map/ppermute | solution.py:51
  467.2 28.5 %collective-permute-done.6 = f32[1376,256]{1,0:T(8,128)S(1)} collective-permute-done((f32[1376,256]{1,0:T(8,128)S(1)}, f32[1376,256]{1,0:T(8,128)S(1)}, u32[]{:S(2)}, u32[]{:S(2)}) %collective-permute-start.6) | collective-permute-done | bytes 1409056 | tf_op jit(solution)/shard_map/ppermute | solution.py:51
  501.7 101.2 %psum.59 = f32[]{:T(128)} all-reduce(f32[]{:T(128)} %multiply_reduce_fusion), channel_id=1, replica_groups=mesh['tok'=16,'feat'=16] {'tok','feat'}, use_global_device_ids=true, to_apply=%region_5.6 | all-reduce | flops 1 | bytes 8 | tf_op jit(solution)/shard_map/psum | solution.py:42
  606.8 23.5 %all-reduce = (f32[256]{0:T(256)S(1)}, f32[256]{0:T(256)S(1)}) all-reduce(f32[256]{0:T(256)S(1)} %get-tuple-element.3, f32[256]{0:T(256)S(1)} %get-tuple-element.2), channel_id=1, replica_groups=mesh['tok'=16,'feat'=16] {'feat'}, use_global_device_ids=true, to_apply=%region_2.3 | all-reduce | flops 512 | bytes 4096 | tf_op jit(solution)/shard_map/psum | solution.py:26
  632.0 25.5 %psum.61 = f32[256]{0:T(256)S(1)} all-reduce(f32[256]{0:T(256)S(1)} %multiply_reduce_fusion.2), channel_id=1, replica_groups=mesh['tok'=16,'feat'=16] {'feat'}, use_global_device_ids=true, to_apply=%region_9.10 | all-reduce | flops 256 | bytes 2048 | tf_op jit(solution)/shard_map/psum | solution.py:26
  657.5 8.8 convolution_bitcast_fusion.3
  666.3 107.6 %all-reduce.9.cloned.1.call-done = f32[1024,256]{0,1:T(8,128)} async-done(((f32[1024,256]{0,1:T(8,128)}), f32[1024,256]{0,1:T(8,128)}) %all-reduce.9.cloned.1.call-update) | async-done | bytes 1048592 | tf_op jit(solution)/shard_map/psum | solution.py:46
  773.9 6.9 convolution_bitcast_fusion
  782.1 30.4 %collective-permute-done.8 = f32[1376,256]{1,0:T(8,128)S(1)} collective-permute-done((f32[1376,256]{1,0:T(8,128)S(1)}, f32[1376,256]{1,0:T(8,128)S(1)}, u32[]{:S(2)}, u32[]{:S(2)}) %collective-permute-start.8) | collective-permute-done | bytes 1409056 | tf_op jit(solution)/shard_map/ppermute | solution.py:51
  815.4 29.4 %collective-permute-done.9 = f32[1376,256]{1,0:T(8,128)S(1)} collective-permute-done((f32[1376,256]{1,0:T(8,128)S(1)}, f32[1376,256]{1,0:T(8,128)S(1)}, u32[]{:S(2)}, u32[]{:S(2)}) %collective-permute-start.9) | collective-permute-done | bytes 1409056 | tf_op jit(solution)/shard_map/ppermute | solution.py:51
  846.4 28.5 %collective-permute-done.10 = f32[1376,256]{1,0:T(8,128)S(1)} collective-permute-done((f32[1376,256]{1,0:T(8,128)S(1)}, f32[1376,256]{1,0:T(8,128)S(1)}, u32[]{:S(2)}, u32[]{:S(2)}) %collective-permute-start.10) | collective-permute-done | bytes 1409056 | tf_op jit(solution)/shard_map/ppermute | solution.py:51
  877.9 29.3 %collective-permute-done.11 = f32[1376,256]{1,0:T(8,128)S(1)} collective-permute-done((f32[1376,256]{1,0:T(8,128)S(1)}, f32[1376,256]{1,0:T(8,128)S(1)}, u32[]{:S(2)}, u32[]{:S(2)}) %collective-permute-start.11) | collective-permute-done | bytes 1409056 | tf_op jit(solution)/shard_map/ppermute | solution.py:51
  908.9 29.2 %psum.63 = f32[256]{0:T(256)S(1)} all-reduce(f32[256]{0:T(256)S(1)} %multiply_reduce_fusion.1), channel_id=1, replica_groups=mesh['tok'=16,'feat'=16] {'feat'}, use_global_device_ids=true, to_apply=%region_12.13 | all-reduce | flops 256 | bytes 2048 | tf_op jit(solution)/shard_map/psum | solution.py:62
  (64 shorter events, 49.1 us)
Async XLA Ops:
  7.2 124.7 %all-reduce.5.cloned.1.call-start = ((), (), s32[]{:S(2)}) async-start(), calls=%async_computation | async-start | bytes 2097152 | tf_op jit(solution)/shard_map/psum | solution.py:46
  16.5 378.0 %all-reduce.7.cloned.1.call-start = ((), (), s32[]{:S(2)}) async-start(), calls=%async_computation.1 | async-start | bytes 2097152 | tf_op jit(solution)/shard_map/psum | solution.py:46
  138.7 31.7 %collective-permute-start = (f32[1376,256]{1,0:T(8,128)S(1)}, f32[1376,256]{1,0:T(8,128)S(1)}, u32[]{:S(2)}, u32[]{:S(2)}) collective-permute-start(f32[1376,256]{1,0:T(8,128)S(1)} %convolution_bitcast_fusion.2), channel_id=1, source_target_pairs={{0,16},{16,0},{32,48},{48,32},{64,80},{80,64},{96,112},{112,96},{1... | collective-permute-start | bytes 4227080 | tf_op jit(solution)/shard_map/ppermute | solution.py:51
  170.6 32.2 %collective-permute-start.1 = (f32[1376,256]{1,0:T(8,128)S(1)}, f32[1376,256]{1,0:T(8,128)S(1)}, u32[]{:S(2)}, u32[]{:S(2)}) collective-permute-start(f32[1376,256]{1,0:T(8,128)S(1)} %add.81), channel_id=1, source_target_pairs={{0,32},{16,48},{32,0},{48,16},{64,96},{80,112},{96,64},{112,80},{1... | collective-permute-start | bytes 4227080 | tf_op jit(solution)/shard_map/ppermute | solution.py:51
  203.0 29.8 %collective-permute-start.2 = (f32[1376,256]{1,0:T(8,128)S(1)}, f32[1376,256]{1,0:T(8,128)S(1)}, u32[]{:S(2)}, u32[]{:S(2)}) collective-permute-start(f32[1376,256]{1,0:T(8,128)S(1)} %add.82), channel_id=1, source_target_pairs={{0,64},{16,80},{32,96},{48,112},{64,0},{80,16},{96,32},{112,48},{1... | collective-permute-start | bytes 4227080 | tf_op jit(solution)/shard_map/ppermute | solution.py:51
  232.8 38.0 %slice-start = ((s8[5636096]{0:T(1024)(128)(4,1)}), s8[1441792]{0:T(1024)(128)(4,1)S(1)}, s32[]{:S(2)}) async-start(s8[5636096]{0:T(1024)(128)(4,1)} %bitcast.35), calls=%async_computation.3 | async-start | bytes 2883584
  233.0 35.2 %copy-start.5 = (f32[1376,256]{1,0:T(8,128)}, f32[1376,256]{1,0:T(8,128)S(1)}, u32[]{:S(2)}) copy-start(f32[1376,256]{1,0:T(8,128)S(1)} %add.83) | copy-start | bytes 4227076
  233.0 32.0 %collective-permute-start.3 = (f32[1376,256]{1,0:T(8,128)S(1)}, f32[1376,256]{1,0:T(8,128)}, u32[]{:S(2)}, u32[]{:S(2)}) collective-permute-start(f32[1376,256]{1,0:T(8,128)S(1)} %add.83), channel_id=1, source_target_pairs={{0,128},{16,144},{32,160},{48,176},{64,192},{80,208},{96,224},{112... | collective-permute-start | bytes 4227080 | tf_op jit(solution)/shard_map/ppermute | solution.py:51
  237.5 33.3 %slice-start.1 = ((s8[5636096]{0:T(1024)(128)(4,1)}), s8[4194304]{0:T(1024)(128)(4,1)S(1)}, s32[]{:S(2)}) async-start(s8[5636096]{0:T(1024)(128)(4,1)} %bitcast.35), calls=%async_computation.4 | async-start | bytes 8388608
  268.2 2.7 copy-start.1
  277.2 496.7 %all-reduce.9.cloned.1.call-start = ((), (), s32[]{:S(2)}) async-start(), calls=%async_computation.2 | async-start | bytes 2097152 | tf_op jit(solution)/shard_map/psum | solution.py:46
  401.4 31.6 %collective-permute-start.4 = (f32[1376,256]{1,0:T(8,128)S(1)}, f32[1376,256]{1,0:T(8,128)S(1)}, u32[]{:S(2)}, u32[]{:S(2)}) collective-permute-start(f32[1376,256]{1,0:T(8,128)S(1)} %convolution_bitcast_fusion.1), channel_id=1, source_target_pairs={{0,16},{16,0},{32,48},{48,32},{64,80},{80,64},{96,112},{112,96},{1... | collective-permute-start | bytes 4227080 | tf_op jit(solution)/shard_map/ppermute | solution.py:51
  433.1 66.6 %slice-start.2 = ((s8[5636096]{0:T(1024)(128)(4,1)}), s8[4194304]{0:T(1024)(128)(4,1)S(1)}, s32[]{:S(2)}) async-start(s8[5636096]{0:T(1024)(128)(4,1)} %bitcast.37), calls=%async_computation.5 | async-start | bytes 8388608
  433.2 66.4 %slice-start.3 = ((s8[5636096]{0:T(1024)(128)(4,1)}), s8[1441792]{0:T(1024)(128)(4,1)S(1)}, s32[]{:S(2)}) async-start(s8[5636096]{0:T(1024)(128)(4,1)} %bitcast.37), calls=%async_computation.6 | async-start | bytes 2883584
  433.2 32.2 %collective-permute-start.5 = (f32[1376,256]{1,0:T(8,128)S(1)}, f32[1376,256]{1,0:T(8,128)S(1)}, u32[]{:S(2)}, u32[]{:S(2)}) collective-permute-start(f32[1376,256]{1,0:T(8,128)S(1)} %add.85), channel_id=1, source_target_pairs={{0,32},{16,48},{32,0},{48,16},{64,96},{80,112},{96,64},{112,80},{1... | collective-permute-start | bytes 4227080 | tf_op jit(solution)/shard_map/ppermute | solution.py:51
  465.7 30.0 %collective-permute-start.6 = (f32[1376,256]{1,0:T(8,128)S(1)}, f32[1376,256]{1,0:T(8,128)S(1)}, u32[]{:S(2)}, u32[]{:S(2)}) collective-permute-start(f32[1376,256]{1,0:T(8,128)S(1)} %add.86), channel_id=1, source_target_pairs={{0,64},{16,80},{32,96},{48,112},{64,0},{80,16},{96,32},{112,48},{1... | collective-permute-start | bytes 4227080 | tf_op jit(solution)/shard_map/ppermute | solution.py:51
  497.0 106.6 %copy-start.2 = (f32[1376,2,128]{2,1,0:T(2,128)S(1)}, f32[1376,2,128]{2,1,0:T(2,128)}, u32[]{:S(2)}) copy-start(f32[1376,2,128]{2,1,0:T(2,128)} %copy-done.1) | copy-start | bytes 4227076
  497.0 106.6 %collective-permute-start.7 = (f32[1376,256]{1,0:T(8,128)}, f32[1376,256]{1,0:T(8,128)}, u32[]{:S(2)}, u32[]{:S(2)}) collective-permute-start(f32[1376,256]{1,0:T(8,128)} %add.87), channel_id=1, source_target_pairs={{0,128},{16,144},{32,160},{48,176},{64,192},{80,208},{96,224},{112... | collective-permute-start | bytes 4227080 | tf_op jit(solution)/shard_map/ppermute | solution.py:51
  780.8 31.6 %collective-permute-start.8 = (f32[1376,256]{1,0:T(8,128)S(1)}, f32[1376,256]{1,0:T(8,128)S(1)}, u32[]{:S(2)}, u32[]{:S(2)}) collective-permute-start(f32[1376,256]{1,0:T(8,128)S(1)} %convolution_bitcast_fusion), channel_id=1, source_target_pairs={{0,16},{16,0},{32,48},{48,32},{64,80},{80,64},{96,112},{112,96},{1... | collective-permute-start | bytes 4227080 | tf_op jit(solution)/shard_map/ppermute | solution.py:51
  812.7 32.2 %collective-permute-start.9 = (f32[1376,256]{1,0:T(8,128)S(1)}, f32[1376,256]{1,0:T(8,128)S(1)}, u32[]{:S(2)}, u32[]{:S(2)}) collective-permute-start(f32[1376,256]{1,0:T(8,128)S(1)} %add.91), channel_id=1, source_target_pairs={{0,32},{16,48},{32,0},{48,16},{64,96},{80,112},{96,64},{112,80},{1... | collective-permute-start | bytes 4227080 | tf_op jit(solution)/shard_map/ppermute | solution.py:51
  845.1 63.3 %copy-start.3 = (f32[1376,256]{1,0:T(8,128)S(1)}, f32[1376,256]{1,0:T(8,128)}, u32[]{:S(2)}) copy-start(f32[1376,256]{1,0:T(8,128)} %get-tuple-element.6) | copy-start | bytes 4227076
  845.1 29.8 %collective-permute-start.10 = (f32[1376,256]{1,0:T(8,128)S(1)}, f32[1376,256]{1,0:T(8,128)S(1)}, u32[]{:S(2)}, u32[]{:S(2)}) collective-permute-start(f32[1376,256]{1,0:T(8,128)S(1)} %add.92), channel_id=1, source_target_pairs={{0,64},{16,80},{32,96},{48,112},{64,0},{80,16},{96,32},{112,48},{1... | collective-permute-start | bytes 4227080 | tf_op jit(solution)/shard_map/ppermute | solution.py:51
  875.1 32.2 %copy-start.4 = (f32[1376,256]{1,0:T(8,128)}, f32[1376,256]{1,0:T(8,128)S(1)}, u32[]{:S(2)}) copy-start(f32[1376,256]{1,0:T(8,128)S(1)} %add.93) | copy-start | bytes 4227076
  875.1 32.2 %collective-permute-start.11 = (f32[1376,256]{1,0:T(8,128)S(1)}, f32[1376,256]{1,0:T(8,128)S(1)}, u32[]{:S(2)}, u32[]{:S(2)}) collective-permute-start(f32[1376,256]{1,0:T(8,128)S(1)} %add.93), channel_id=1, source_target_pairs={{0,128},{16,144},{32,160},{48,176},{64,192},{80,208},{96,224},{112... | collective-permute-start | bytes 4227080 | tf_op jit(solution)/shard_map/ppermute | solution.py:51
  (2 other events, 2.2 us)
Sparse Core Ops, SparseCore 0:
  16.6 115.1 all-reduce.4
  277.4 117.0 all-reduce.6
  666.4 107.4 all-reduce.8
